TPU v7x, 32 devices: a whole 2x2x4 slice. The times are simulated.
32 devices in a mesh: pipe: 8 (over z, core), tensor: 4 (over y, x).
Axes of the slice: x: 2, y: 2, z: 4, core: 2. Of those that a mesh axis runs over, the one named last changes fastest.
Arguments:
- held_rows: bfloat16 [8, 512, 2688], P('pipe', 'tensor'), may hold values from -6 to 6
- incoming: bfloat16 [1, 512, 2688], P(None, 'tensor'), may hold values from -6 to 6
- first_position: int32 [1], replicated, may hold values from 0 to 511
- in_gain: float32 [8, 2688], P('pipe'), may hold values from 0.5 to 1.5
- query_key_value_weight: bfloat16 [8, 2688, 16, 512], P('pipe', None, 'tensor'), may hold values from -0.125 to 0.125
- q_gain: float32 [8, 128], P('pipe'), may hold values from 0.5 to 1.5
- k_gain: float32 [8, 128], P('pipe'), may hold values from 0.5 to 1.5
- cached_key_rows: bfloat16 [8, 16, 1024, 128], P('pipe', 'tensor'), may hold values from -3 to 3
- cached_value_rows: bfloat16 [8, 16, 1024, 128], P('pipe', 'tensor'), may hold values from -6 to 6
- w_out: bfloat16 [8, 4096, 2688], P('pipe', 'tensor'), may hold values from -0.09375 to 0.09375
- post_gain: float32 [8, 2688], P('pipe'), may hold values from 0.5 to 1.5
Outputs:
- hidden: bfloat16 [8, 2, 512, 2688], P('pipe', None, 'tensor')
All inputs are finite; a program needn't handle non-finite values.
Results may differ from a plain program's by a relative error of at most 0.015.
Values may be sent and summed in bfloat16 or wider, within the bound.
No kernel may reach another device: no remote copies, remote signals or barrier semaphores. Data moves between devices by JAX's collectives and lax.ppermute only.
A program may use at most 128 MiB of HBM per device.

v0:
```python
import math
import jax
import jax.numpy as jnp
from jax import lax
from jax.sharding import PartitionSpec as P

HEAD_SIZE = 128
WINDOW_LENGTH = 1024
TICKS = 2
ROWS = 512
query_scale = 168.0 ** (-0.5)
norm_eps = 1e-06
rope_base = 10000.0


def shifted(block, axis, distance):
    devices = range(lax.axis_size(axis))
    route = [(i - distance, i) for i in devices if i - distance in devices]
    return lax.ppermute(block, axis, route)


def rms_scale(values, gain_vec):
    mean_square = jnp.mean(values * values, axis=-1, keepdims=True)
    return values * lax.rsqrt(mean_square + norm_eps) * gain_vec


def rotate(values, positions):
    half_width = values.shape[-1] // 2
    frequency = jnp.exp(
        jnp.arange(half_width, dtype=jnp.float32) * (-math.log(rope_base) / half_width)
    )
    angles = positions.astype(jnp.float32)[:, None] * frequency[None, :]
    angles = angles.reshape((angles.shape[0],) + (1,) * (values.ndim - 2) + (half_width,))
    cosine = jnp.cos(angles)
    sine_part = jnp.sin(angles)
    first_half = values[..., :half_width]
    second = values[..., half_width:]
    return jnp.concatenate(
        [first_half * cosine - second * sine_part, second * cosine + first_half * sine_part],
        axis=-1,
    )


def attend(projected_rows, prev_keys, prev_values, start_pos, q_scale, k_scale):
    row_total = projected_rows.shape[0]
    kv_local = prev_keys.shape[0]
    group_size = projected_rows.shape[1] // (kv_local * HEAD_SIZE) - 2
    blocks = projected_rows.reshape(row_total, kv_local, group_size + 2, HEAD_SIZE)
    query_pos = start_pos + jnp.arange(row_total, dtype=jnp.int32)
    queries = rotate(rms_scale(blocks[:, :, :group_size], q_scale), query_pos).astype(jnp.bfloat16)
    key_rows = rotate(rms_scale(blocks[:, :, group_size], k_scale), query_pos).astype(jnp.bfloat16)
    value_rows = blocks[:, :, group_size + 1].astype(jnp.bfloat16)
    key_heads = jnp.swapaxes(key_rows, 0, 1)
    value_heads = jnp.swapaxes(value_rows, 0, 1)
    all_keys = jnp.concatenate([prev_keys, key_heads], axis=1)
    all_values = jnp.concatenate([prev_values, value_heads], axis=1)
    prev_length = prev_keys.shape[1]
    key_pos = start_pos - prev_length + jnp.arange(prev_length + row_total, dtype=jnp.int32)
    visible = (
        (key_pos[None, :] <= query_pos[:, None])
        & (key_pos[None, :] > query_pos[:, None] - WINDOW_LENGTH)
        & (key_pos[None, :] >= 0)
    )
    scores = (
        jnp.einsum("rkgd,kld->kgrl", queries, all_keys, preferred_element_type=jnp.float32)
        * query_scale
    )
    weights = jnp.where(visible[None, None], jnp.exp(scores), 0.0)
    totals = jnp.sum(weights, axis=-1, keepdims=True)
    mixed_heads = (
        jnp.einsum(
            "kgrl,kld->kgrd",
            weights.astype(jnp.bfloat16),
            all_values,
            preferred_element_type=jnp.float32,
        )
        / totals
    )
    mixed_heads = jnp.transpose(mixed_heads.astype(jnp.bfloat16), (2, 0, 1, 3)).reshape(
        row_total, -1
    )
    return (mixed_heads, key_heads, value_heads)


def shards(
    held_rows,
    incoming,
    first_position,
    in_gain,
    query_key_value_weight,
    q_gain,
    k_gain,
    cached_key_rows,
    cached_value_rows,
    w_out,
    post_gain,
):
    section_id = lax.axis_index("pipe")
    section_count = lax.axis_size("pipe")
    model_width = held_rows.shape[2]
    in_scale = in_gain[0]
    post_scale = post_gain[0]
    q_scale = q_gain[0]
    k_scale = k_gain[0]
    w_flat = query_key_value_weight[0].reshape(model_width, -1)
    w_local = w_out[0]
    prev_keys = cached_key_rows[0]
    prev_values = cached_value_rows[0]
    outputs = []
    current = held_rows[0]
    for micro_step in range(TICKS):
        start_pos = first_position[0] + (section_count - 1 - section_id + micro_step) * ROWS
        projected_rows = jnp.dot(
            (
                lax.all_gather(current, "tensor", axis=0, tiled=True).astype(jnp.float32) * in_scale
            ).astype(jnp.bfloat16),
            w_flat,
            preferred_element_type=jnp.float32,
        )
        mixed_heads, key_heads, value_heads = attend(
            projected_rows, prev_keys, prev_values, start_pos, q_scale, k_scale
        )
        summed = lax.psum_scatter(
            jnp.dot(mixed_heads, w_local, preferred_element_type=jnp.float32).astype(jnp.bfloat16),
            "tensor",
            scatter_dimension=0,
            tiled=True,
        ).astype(jnp.float32)
        hidden = (current.astype(jnp.float32) + rms_scale(summed, post_scale)).astype(jnp.bfloat16)
        outputs.append(hidden)
        if micro_step + 1 < TICKS:
            prev_keys = jnp.concatenate([prev_keys, key_heads], axis=1)
            prev_values = jnp.concatenate([prev_values, value_heads], axis=1)
            passed = shifted(hidden, "pipe", 1)
            current = jnp.where(section_id == 0, incoming[micro_step], passed)
    return jnp.stack(outputs, axis=0)[None]


def solution(mesh):
    return jax.shard_map(
        shards,
        mesh=mesh,
        in_specs=(
            P("pipe", "tensor", None),
            P(None, "tensor", None),
            P(),
            P("pipe", None),
            P("pipe", None, "tensor", None),
            P("pipe", None),
            P("pipe", None),
            P("pipe", "tensor", None, None),
            P("pipe", "tensor", None, None),
            P("pipe", "tensor", None),
            P("pipe", None),
        ),
        out_specs=P("pipe", None, "tensor", None),
        check_vma=False,
    )
```

profile of v0, /device:TPU:0, one launch (start us, length us, event | category | flops | bytes accessed | tf_op | source)
XLA Modules:
  0.0 297.5 jit_solution(13383296722176563755)
XLA Ops:
  6.5 0.7 all-gather.6.cloned.1.call-update
  8.0 1.5 copy.15
  9.4 12.3 %copy.35 = bf16[336,8,4,512]{3,1,2,0:T(8,128)(2,1)} copy(bf16[336,8,4,512]{3,2,1,0:T(4,128)(2,1)} %bitcast.133) | data formatting | bytes 22020096
  21.7 14.2 %copy.12 = bf16[2048,2688]{1,0:T(8,128)(2,1)} copy(bf16[2048,2688]{0,1:T(8,128)(2,1)} %bitcast.132) | data formatting | bytes 22020096 | tf_op jit(solution)/shard_map/dot_general | solution.py:113
  36.0 1.0 multiply_cosine_fusion
  37.0 1.1 and_and_fusion.1
  38.1 14.4 %all-gather.6.cloned.1.call-done = bf16[1,512,2688]{2,1,0:T(8,128)(2,1)} async-done(((bf16[1,128,2688]{2,1,0:T(8,128)(2,1)}), bf16[1,512,2688]{2,1,0:T(8,128)(2,1)}) %all-gather.6.cloned.1.call-update) | async-done | bytes 2752528 | tf_op jit(solution)/shard_map/all_gather | solution.py:115
  52.5 9.8 %fusion.27 = f32[512,4,4,128]{0,3,2,1:T(8,128)S(1)} fusion(bf16[4,4,128,2688]{3,2,1,0:T(8,128)(2,1)} %bitcast.134, bf16[1,512,2688]{2,1,0:T(8,128)(2,1)} %all-gather.6.cloned.1.call-done, f32[2688]{0:T(1024)S(1)} %reduce), kind=kOutput, calls=%fused_computation.26 | convolution fusion | flops 5641273344 | bytes 17967616 | tf_op jit(solution)/shard_map/dot_general | solution.py:113
  62.7 0.9 fusion.67
  64.4 1.3 subtract_convert_fusion.1
  66.2 12.5 %fusion.2 = (f32[4,2,512]{2,1,0:T(2,128)S(1)}, f32[4,1536,512,2]{2,1,3,0:T(8,128)}) fusion(pred[512,1536]{0,1:T(8,128)(4,1)S(1)} %and_and_fusion.1, bf16[512,4,2,64]{0,3,2,1:T(8,128)(2,1)} %get-tuple-element.8, bf16[512,4,2,64]{0,3,2,1:T(8,128)(2,1)} %get-tuple-element.7, bf16[4,512,128]{2,1,0:T(8,128)(2,1)S(1)} %copy.13, bf16[4,1024,128]{2,1,0:T(8,128)(2,1)} %bitcast.145), kind=kOutput, calls=%fused_computation.4 | convolution fusion | flops 1634725888 | bytes 28590080 | tf_op jit(solution)/shard_map/rkgd,kld->kgrl/dot_general | solution.py:65
  78.8 11.2 %fusion.42 = bf16[512,4,2,128]{0,3,2,1:T(8,128)(2,1)S(1)} fusion(f32[4,1536,512,2]{2,1,3,0:T(8,128)} %get-tuple-element.20, pred[512,1536]{0,1:T(8,128)(4,1)S(1)} %and_and_fusion.1, bf16[4,512,128]{1,2,0:T(8,128)(2,1)S(1)} %copy-done.3, bf16[4,1024,128]{1,2,0:T(8,128)(2,1)S(1)} %bitcast.137, f32[512,4,2]{0,2,1:T(2,128)S(1)} %bitcast.150), kind=kOutput, calls=%fused_computation.44 | convolution fusion | flops 1633681408 | bytes 28590080 | tf_op jit(solution)/shard_map/kgrl,kld->kgrd/dot_general | solution.py:71
  90.0 4.5 %fusion.17 = bf16[512,2688]{1,0:T(8,128)(2,1)} fusion(bf16[512,1024]{0,1:T(8,128)(2,1)S(1)} %bitcast.148, bf16[1,1024,2688]{2,1,0:T(8,128)(2,1)S(1)} %bitcast.144), kind=kOutput, calls=%fused_computation.19 | convolution fusion | flops 2819948544 | bytes 9306112 | tf_op jit(solution)/shard_map/dot_general | solution.py:124
  94.6 40.7 %reduce-scatter.3.cloned.1.call-done = bf16[128,2688]{1,0:T(8,128)(2,1)} async-done(((bf16[512,2688]{1,0:T(8,128)(2,1)}), bf16[128,2688]{1,0:T(8,128)(2,1)}) %reduce-scatter.3.cloned.1.call-update) | async-done | bytes 688144 | tf_op jit(solution)/shard_map/reduce_scatter | solution.py:123
  135.3 1.3 fusion.52
  136.7 1.4 fusion.55
  138.1 1.6 collective-permute-start
  139.7 1.7 collective-permute-done
  141.4 0.9 bitcast_select_fusion.2
  142.5 2.5 and_and_fusion
  145.0 47.1 %all-gather.4.cloned.1.call-done = bf16[512,2688]{1,0:T(8,128)(2,1)} async-done(((bf16[128,2688]{1,0:T(8,128)(2,1)}), bf16[512,2688]{1,0:T(8,128)(2,1)}) %all-gather.4.cloned.1.call-update) | async-done | bytes 2752528 | tf_op jit(solution)/shard_map/all_gather | solution.py:115
  192.0 9.8 %fusion.24 = f32[512,4,4,128]{0,3,2,1:T(8,128)S(1)} fusion(bf16[4,4,128,2688]{3,2,1,0:T(8,128)(2,1)} %bitcast.135, bf16[512,2688]{1,0:T(8,128)(2,1)} %all-gather.4.cloned.1.call-done, f32[2688]{0:T(1024)S(1)} %reduce), kind=kOutput, calls=%fused_computation.24 | convolution fusion | flops 5641273344 | bytes 17967616 | tf_op jit(solution)/shard_map/dot_general | solution.py:113
  202.2 0.9 fusion.68
  203.8 1.4 subtract_convert_fusion
  205.4 1.0 copy.19
  206.4 17.0 %fusion = (f32[4,2,512]{2,1,0:T(2,128)S(1)}, f32[4,2048,512,2]{2,1,3,0:T(8,128)}) fusion(pred[512,2048]{0,1:T(8,128)(4,1)} %and_and_fusion, bf16[512,4,2,64]{0,3,2,1:T(8,128)(2,1)} %get-tuple-element.6, bf16[512,4,2,64]{0,3,2,1:T(8,128)(2,1)} %get-tuple-element.5, bf16[4,512,128]{2,1,0:T(8,128)(2,1)} %copy.19, bf16[4,512,128]{2,1,0:T(8,128)(2,1)S(1)} %copy-done.6, ...), kind=kOutput, calls=%fused_computation.1 | convolution fusion | flops 2181033984 | bytes 37765120 | tf_op jit(solution)/shard_map/rkgd,kld->kgrl/dot_general | solution.py:65
  223.3 15.1 %fusion.41 = bf16[512,4,2,128]{0,3,2,1:T(8,128)(2,1)} fusion(f32[4,2048,512,2]{2,1,3,0:T(8,128)} %get-tuple-element.22, pred[512,2048]{0,1:T(8,128)(4,1)} %and_and_fusion, bf16[4,512,128]{1,2,0:T(8,128)(2,1)} %fusion.68, bf16[4,512,128]{1,2,0:T(8,128)(2,1)S(1)} %copy-done.4, bf16[4,1024,128]{1,2,0:T(8,128)(2,1)S(1)} %bitcast.138, f32[512,4,2]{0,2,1:T(2,128)S(1)} %bitcast.149), kind=kOutput, calls=%fused_computation.42 | convolution fusion | flops 2179989504 | bytes 37765120 | tf_op jit(solution)/shard_map/kgrl,kld->kgrd/dot_general | solution.py:71
  238.5 7.7 %fusion.20 = bf16[512,2688]{1,0:T(8,128)(2,1)} fusion(bf16[512,1024]{0,1:T(8,128)(2,1)} %bitcast.147, bf16[1,1024,2688]{2,1,0:T(8,128)(2,1)} %param.20), kind=kOutput, calls=%fused_computation.20 | convolution fusion | flops 2819948544 | bytes 9306112 | tf_op jit(solution)/shard_map/dot_general | solution.py:124
  246.1 40.8 %reduce-scatter.5.cloned.1.call-done = bf16[128,2688]{1,0:T(8,128)(2,1)} async-done(((bf16[512,2688]{1,0:T(8,128)(2,1)}), bf16[128,2688]{1,0:T(8,128)(2,1)}) %reduce-scatter.5.cloned.1.call-update) | async-done | bytes 688144 | tf_op jit(solution)/shard_map/reduce_scatter | solution.py:123
  286.9 1.3 fusion.56
  288.3 1.4 fusion.66
  289.7 1.2 maximum_bitcast_fusion.10
  (63 shorter events, 3.2 us)
Async XLA Ops:
  6.5 46.0 %all-gather.6.cloned.1.call-start = ((), (), s32[]{:S(2)}) async-start(), calls=%async_computation.5 | async-start | bytes 3440640 | tf_op jit(solution)/shard_map/all_gather | solution.py:115
  7.3 128.1 %reduce-scatter.3.cloned.1.call-start = ((), (), s32[]{:S(2)}) async-start(), calls=%async_computation.2 | async-start | bytes 3440640 | tf_op jit(solution)/shard_map/reduce_scatter | solution.py:123
  21.7 14.2 %copy-start.7 = (f32[1,2688]{1,0:T(1,128)S(1)}, f32[1,2688]{1,0:T(1,128)}, u32[]{:S(2)}) copy-start(f32[1,2688]{1,0:T(1,128)} %param.14) | copy-start | bytes 32260
  62.3 1.4 copy-start.9
  62.3 1.6 copy-start.10
  66.2 12.5 %copy-start.5 = (bf16[4,512,128]{2,1,0:T(8,128)(2,1)}, bf16[4,512,128]{2,1,0:T(8,128)(2,1)S(1)}, u32[]{:S(2)}) copy-start(bf16[4,512,128]{2,1,0:T(8,128)(2,1)S(1)} %copy.13) | copy-start | bytes 1572868
  66.2 12.5 %copy-start.3 = (bf16[4,512,128]{1,2,0:T(8,128)(2,1)S(1)}, bf16[4,512,128]{1,2,0:T(8,128)(2,1)}, u32[]{:S(2)}) copy-start(bf16[4,512,128]{1,2,0:T(8,128)(2,1)} %fusion.67) | copy-start | bytes 1572868
  66.2 23.7 %slice-start = ((s8[5505024]{0:T(1024)(128)(4,1)}), s8[4194304]{0:T(1024)(128)(4,1)S(1)}, s32[]{:S(2)}) async-start(s8[5505024]{0:T(1024)(128)(4,1)} %bitcast.143), calls=%async_computation.6 | async-start | bytes 8388608
  78.8 11.2 %slice-start.1 = ((s8[5505024]{0:T(1024)(128)(4,1)}), s8[1310720]{0:T(1024)(128)(4,1)S(1)}, s32[]{:S(2)}) async-start(s8[5505024]{0:T(1024)(128)(4,1)} %bitcast.143), calls=%async_computation.7 | async-start | bytes 2621440
  90.0 4.6 %copy-start.8 = (f32[1,2688]{1,0:T(1,128)S(1)}, f32[1,2688]{1,0:T(1,128)}, u32[]{:S(2)}) copy-start(f32[1,2688]{1,0:T(1,128)} %param.21) | copy-start | bytes 32260
  94.5 42.2 %copy-start.1 = (bf16[1,128,2688]{2,1,0:T(8,128)(2,1)S(1)}, bf16[1,128,2688]{2,1,0:T(8,128)(2,1)}, u32[]{:S(2)}) copy-start(bf16[1,128,2688]{2,1,0:T(8,128)(2,1)} %param.11) | copy-start | bytes 2064388
  94.5 46.9 %copy-start.2 = (bf16[1,128,2688]{2,1,0:T(8,128)(2,1)S(1)}, bf16[1,128,2688]{2,1,0:T(8,128)(2,1)}, u32[]{:S(2)}) copy-start(bf16[1,128,2688]{2,1,0:T(8,128)(2,1)} %param.12) | copy-start | bytes 2064388
  94.6 97.5 %all-gather.4.cloned.1.call-start = ((), (), s32[]{:S(2)}) async-start(), calls=%async_computation.3 | async-start | bytes 3440640 | tf_op jit(solution)/shard_map/all_gather | solution.py:115
  138.1 3.3 %collective-permute-start = (bf16[128,2688]{1,0:T(8,128)(2,1)S(1)}, bf16[128,2688]{1,0:T(8,128)(2,1)S(1)}, u32[]{:S(2)}, u32[]{:S(2)}) collective-permute-start(bf16[128,2688]{1,0:T(8,128)(2,1)S(1)} %fusion.55), channel_id=1, source_target_pairs={{0,4},{4,8},{8,12},{12,16},{16,20},{20,24},{24,28},{1,5},{5,9},{9,... | collective-permute-start | bytes 2064392 | tf_op jit(solution)/shard_map/ppermute | solution.py:19
  142.4 144.6 %reduce-scatter.5.cloned.1.call-start = ((), (), s32[]{:S(2)}) async-start(), calls=%async_computation.4 | async-start | bytes 3440640 | tf_op jit(solution)/shard_map/reduce_scatter | solution.py:123
  203.8 2.6 copy-start.6
  206.4 17.0 %copy-start.4 = (bf16[4,512,128]{1,2,0:T(8,128)(2,1)S(1)}, bf16[4,512,128]{1,2,0:T(8,128)(2,1)}, u32[]{:S(2)}) copy-start(bf16[4,512,128]{1,2,0:T(8,128)(2,1)} %fusion.67) | copy-start | bytes 1572868
  246.1 42.2 %copy-start = (bf16[128,2688]{1,0:T(8,128)(2,1)S(1)}, bf16[128,2688]{1,0:T(8,128)(2,1)}, u32[]{:S(2)}) copy-start(bf16[128,2688]{1,0:T(8,128)(2,1)} %bitcast_select_fusion.2) | copy-start | bytes 2064388
Sparse Core Ops, SparseCore 0:
  9.2 43.3 all-gather.5
  94.7 40.6 reduce-scatter.2
  142.5 49.5 all-gather.3
  246.3 40.6 reduce-scatter.4
where the time goes:
time: 298 us; the launch traced here: 297 us
  waiting for transfers between devices  145 us (49%)
  matrix products  87.5 us (29%)
  local copies, waits for them, and re-layouts  31.1 us (10%)
  other arithmetic  17.6 us (6%)
  between operations  14.2 us (5%)
    reduce_scatter x2, waiting for transfers between devices, shards(): lax.psum_scatter(jnp.dot(mixed_heads, w_local, preferred_element_type=jnp...  81.5 us
    all_gather x2, waiting for transfers between devices, shards(): lax.all_gather(current, 'tensor', axis=0, tiled=True).astype(jnp.float32)  61.5 us
    dot_general x2, matrix products, attend(): jnp.einsum('rkgd,kld->kgrl', queries, all_keys, preferred_element_type=jn...  29.5 us
    dot_general x2, matrix products, attend(): jnp.einsum('kgrl,kld->kgrd', weights.astype(jnp.bfloat16), all_values, pr...  26.3 us
    dot_general x2, matrix products, shards(): jnp.dot((lax.all_gather(current, 'tensor', axis=0, tiled=True).astype(jnp...  19.5 us
    dot_general x1, local copies, waits for them, and re-layouts, shards(): jnp.dot((lax.all_gather(current, 'tensor', axis=0, tiled=True).astype(jnp...  14.2 us
    unnamed x28, local copies, waits for them, and re-layouts  13.8 us
    dot_general x2, matrix products, shards(): jnp.dot(mixed_heads, w_local, preferred_element_type=jnp.float32)  12.2 us
  transfers between devices with their start and end apart: 5, of which 5 were waited for; matrix products, arithmetic and copies ran while one was open for 11% of the time, Pallas kernels for 0%

commit v1 on v0

--- a/solution.py
+++ b/solution.py
@@ -11,6 +11,28 @@
 query_scale = 168.0 ** (-0.5)
 norm_eps = 1e-06
 rope_base = 10000.0
+
+
+def laid_out(blocks, dim):
+    blocks = jnp.moveaxis(blocks, 0, dim)
+    shape = blocks.shape
+    return blocks.reshape(*shape[:dim], shape[dim] * shape[dim + 1], *shape[dim + 2 :])
+
+
+def gather_around(array, axis, dim):
+    size = lax.axis_size(axis)
+    pairs = [(i, (i + 1) % size) for i in range(size)]
+    back = [(b, a) for a, b in pairs]
+    lower, upper = ([], [])
+    for hop in range(size - 1):
+        if hop % 2 == 0:
+            lower.append(lax.ppermute(lower[-1] if lower else array, axis, pairs))
+        else:
+            upper.append(lax.ppermute(upper[-1] if upper else array, axis, back))
+    blocks = jnp.stack([*lower[::-1], array, *upper])
+    shift = lax.axis_index(axis) - len(lower)
+    blocks = blocks[(jnp.arange(size) - shift) % size]
+    return laid_out(blocks, dim)
 
 
 def shifted(block, axis, distance):
@@ -111,9 +133,9 @@
     for micro_step in range(TICKS):
         start_pos = first_position[0] + (section_count - 1 - section_id + micro_step) * ROWS
         projected_rows = jnp.dot(
-            (
-                lax.all_gather(current, "tensor", axis=0, tiled=True).astype(jnp.float32) * in_scale
-            ).astype(jnp.bfloat16),
+            (gather_around(current, "tensor", 0).astype(jnp.float32) * in_scale).astype(
+                jnp.bfloat16
+            ),
             w_flat,
             preferred_element_type=jnp.float32,
         )

time: 298 us -> 320 us (1.074)
  starting transfers between devices: 1.74 us -> 10.4 us
  other arithmetic: 17.6 us -> 25.8 us
  local copies, waits for them, and re-layouts: 31.1 us -> 37.5 us
    all_gather x2 -> x0, waiting for transfers between devices: 61.5 us -> none  [shards(): lax.all_gather(current, 'tensor', axis=0, tiled=True).astype(jnp.float32)]
    ppermute x0 -> x6, waiting for transfers between devices: none -> 48.7 us  [the longest x4 37.1 us: gather_around(): lower.append(lax.ppermute(lower[-1] if lower else array, axis, pairs))]
    reduce_scatter x2, waiting for transfers between devices: 81.5 us -> 94.6 us  [shards(): lax.psum_scatter(jnp.dot(mixed_heads, w_local, preferred_element_type=jnp...]
    ppermute x0 -> x6, starting transfers between devices: none -> 8.77 us  [the longest x4 6.34 us: gather_around(): lower.append(lax.ppermute(lower[-1] if lower else array, axis, pairs))]
    gather x0 -> x2, local copies, waits for them, and re-layouts: none -> 4.72 us  [gather_around(): blocks = blocks[(jnp.arange(size) - shift) % size]]
    convert_element_type x1 -> x2, other arithmetic: 0.01 us -> 4.45 us  [shards(): (gather_around(current, 'tensor', 0).astype(jnp.float32) * in_scale).asty...]
    unnamed x28 -> x50, local copies, waits for them, and re-layouts: 13.8 us -> 16.5 us
  transfers between devices with their start and end apart: 5 -> 9, of which waited for: 5 -> 7; matrix products, arithmetic and copies ran while one was open for 11% -> 11% of each run, Pallas kernels for 0% -> 0%
where the time goes in v1:
time: 320 us; the launch traced here: 319 us
  waiting for transfers between devices  145 us (45%)
  matrix products  85.6 us (27%)
  local copies, waits for them, and re-layouts  37.5 us (12%)
  other arithmetic  25.8 us (8%)
  between operations  14.5 us (5%)
  starting transfers between devices  10.4 us (3%)
    reduce_scatter x2, waiting for transfers between devices, shards(): lax.psum_scatter(jnp.dot(mixed_heads, w_local, preferred_element_type=jnp...  94.6 us
    ppermute x4, waiting for transfers between devices, gather_around(): lower.append(lax.ppermute(lower[-1] if lower else array, axis, pairs))  37.1 us
    dot_general x2, matrix products, attend(): jnp.einsum('rkgd,kld->kgrl', queries, all_keys, preferred_element_type=jn...  29.2 us
    dot_general x2, matrix products, attend(): jnp.einsum('kgrl,kld->kgrd', weights.astype(jnp.bfloat16), all_values, pr...  26.1 us
    dot_general x2, matrix products, shards(): jnp.dot((gather_around(current, 'tensor', 0).astype(jnp.float32) * in_sca...  17.9 us
    unnamed x50, local copies, waits for them, and re-layouts  16.5 us
    dot_general x1, local copies, waits for them, and re-layouts, shards(): jnp.dot((gather_around(current, 'tensor', 0).astype(jnp.float32) * in_sca...  14.1 us
    dot_general x2, matrix products, shards(): jnp.dot(mixed_heads, w_local, preferred_element_type=jnp.float32)  12.3 us
  transfers between devices with their start and end apart: 9, of which 7 were waited for; matrix products, arithmetic and copies ran while one was open for 11% of the time, Pallas kernels for 0%

profile of v1, /device:TPU:0, one launch (start us, length us, event | category | flops | bytes accessed | tf_op | source)
XLA Modules:
  0.0 318.8 jit_solution(2927062476415241471)
XLA Ops:
  6.5 3.0 collective-permute-start
  11.1 2.3 copy.15
  13.5 12.1 %copy.35 = bf16[336,8,4,512]{3,1,2,0:T(8,128)(2,1)} copy(bf16[336,8,4,512]{3,2,1,0:T(4,128)(2,1)} %bitcast.137) | data formatting | bytes 22020096
  25.5 14.1 %copy.12 = bf16[2048,2688]{1,0:T(8,128)(2,1)} copy(bf16[2048,2688]{0,1:T(8,128)(2,1)} %bitcast.136) | data formatting | bytes 22020096 | tf_op jit(solution)/shard_map/dot_general | solution.py:135
  41.1 1.8 multiply_cosine_fusion
  42.8 1.8 and_and_fusion.1
  44.7 13.1 %collective-permute-done.1 = bf16[128,2688]{1,0:T(8,128)(2,1)S(1)} collective-permute-done((bf16[128,2688]{1,0:T(8,128)(2,1)S(1)}, bf16[128,2688]{1,0:T(8,128)(2,1)S(1)}, u32[]{:S(2)}, u32[]{:S(2)}) %collective-permute-start.1) | collective-permute-done | bytes 688160 | tf_op jit(solution)/shard_map/ppermute | solution.py:29
  57.8 1.5 pad_maximum_fusion
  59.4 2.4 gather_fusion
  61.7 2.2 multiply_convert_fusion.1
  64.0 8.9 %fusion.73 = f32[512,4,4,128]{0,3,2,1:T(8,128)S(1)} fusion(bf16[512,2688,1,1]{1,0,3,2:T(8,128)(2,1)S(1)} %bitcast.142, bf16[4,4,128,2688]{3,2,1,0:T(8,128)(2,1)} %bitcast.138), kind=kOutput, calls=%fused_computation.129 | convolution fusion | flops 5637144576 | bytes 17956864 | tf_op jit(solution)/shard_map/dot_general | solution.py:135
  77.1 12.4 %fusion.2 = (f32[4,2,512]{2,1,0:T(2,128)S(1)}, f32[4,1536,512,2]{2,1,3,0:T(8,128)}) fusion(pred[512,1536]{0,1:T(8,128)(4,1)S(1)} %copy-done.10, bf16[512,4,2,64]{0,3,2,1:T(8,128)(2,1)} %get-tuple-element.8, bf16[512,4,2,64]{0,3,2,1:T(8,128)(2,1)} %get-tuple-element.7, bf16[4,512,128]{2,1,0:T(8,128)(2,1)S(1)} %copy.13, bf16[4,1024,128]{2,1,0:T(8,128)(2,1)} %bitcast.160), kind=kOutput, calls=%fused_computation.6 | convolution fusion | flops 1634725888 | bytes 28590080 | tf_op jit(solution)/shard_map/rkgd,kld->kgrl/dot_general | solution.py:87
  89.5 11.0 %fusion.32 = bf16[512,4,2,128]{0,3,2,1:T(8,128)(2,1)S(1)} fusion(f32[4,1536,512,2]{2,1,3,0:T(8,128)} %get-tuple-element.20, pred[512,1536]{0,1:T(8,128)(4,1)S(1)} %copy-done.10, bf16[4,512,128]{1,2,0:T(8,128)(2,1)S(1)} %fusion.57, bf16[4,1024,128]{1,2,0:T(8,128)(2,1)S(1)} %bitcast.146, f32[512,4,2]{0,2,1:T(2,128)S(1)} %bitcast.165), kind=kOutput, calls=%fused_computation.40 | convolution fusion | flops 1633681408 | bytes 28590080 | tf_op jit(solution)/shard_map/kgrl,kld->kgrd/dot_general | solution.py:93
  100.6 4.7 %fusion.16 = bf16[512,2688]{1,0:T(8,128)(2,1)} fusion(bf16[512,1024]{0,1:T(8,128)(2,1)S(1)} %bitcast.163, bf16[1,1024,2688]{2,1,0:T(8,128)(2,1)S(1)} %bitcast.159), kind=kOutput, calls=%fused_computation.20 | convolution fusion | flops 2819948544 | bytes 9306112 | tf_op jit(solution)/shard_map/dot_general | solution.py:146
  106.0 40.6 %reduce-scatter.3.cloned.1.call-done = bf16[128,2688]{1,0:T(8,128)(2,1)} async-done(((bf16[512,2688]{1,0:T(8,128)(2,1)}), bf16[128,2688]{1,0:T(8,128)(2,1)}) %reduce-scatter.3.cloned.1.call-update) | async-done | bytes 688144 | tf_op jit(solution)/shard_map/reduce_scatter | solution.py:145
  147.9 1.4 fusion.45
  149.4 1.6 collective-permute-start.3
  151.0 1.7 collective-permute-done.3
  152.8 1.5 collective-permute-start.4
  154.3 1.5 collective-permute-start.6
  155.8 9.2 %collective-permute-done.4 = bf16[128,2688]{1,0:T(8,128)(2,1)S(1)} collective-permute-done((bf16[128,2688]{1,0:T(8,128)(2,1)S(1)}, bf16[128,2688]{1,0:T(8,128)(2,1)S(1)}, u32[]{:S(2)}, u32[]{:S(2)}) %collective-permute-start.4) | collective-permute-done | bytes 688160 | tf_op jit(solution)/shard_map/ppermute | solution.py:29
  165.6 2.5 and_and_fusion
  168.1 11.7 %collective-permute-done.6 = bf16[128,2688]{1,0:T(8,128)(2,1)S(1)} collective-permute-done((bf16[128,2688]{1,0:T(8,128)(2,1)S(1)}, bf16[128,2688]{1,0:T(8,128)(2,1)S(1)}, u32[]{:S(2)}, u32[]{:S(2)}) %collective-permute-start.6) | collective-permute-done | bytes 688160 | tf_op jit(solution)/shard_map/ppermute | solution.py:31
  179.7 14.7 %collective-permute-done.5 = bf16[128,2688]{1,0:T(8,128)(2,1)S(1)} collective-permute-done((bf16[128,2688]{1,0:T(8,128)(2,1)S(1)}, bf16[128,2688]{1,0:T(8,128)(2,1)S(1)}, u32[]{:S(2)}, u32[]{:S(2)}) %collective-permute-start.5) | collective-permute-done | bytes 688160 | tf_op jit(solution)/shard_map/ppermute | solution.py:29
  194.5 1.4 pad_maximum_fusion.1
  195.9 2.4 gather_fusion.1
  198.3 2.2 multiply_convert_fusion
  200.5 8.9 %fusion.74 = f32[512,4,4,128]{0,3,2,1:T(8,128)S(1)} fusion(bf16[512,2688,1,1]{1,0,3,2:T(8,128)(2,1)S(1)} %bitcast.141, bf16[4,4,128,2688]{3,2,1,0:T(8,128)(2,1)} %bitcast.139), kind=kOutput, calls=%fused_computation.130 | convolution fusion | flops 5637144576 | bytes 17956864 | tf_op jit(solution)/shard_map/dot_general | solution.py:135
  214.4 16.7 %fusion = (f32[4,2,512]{2,1,0:T(2,128)S(1)}, f32[4,2048,512,2]{2,1,3,0:T(8,128)}) fusion(pred[512,2048]{0,1:T(8,128)(4,1)S(1)} %copy-done.9, bf16[512,4,2,64]{0,3,2,1:T(8,128)(2,1)} %get-tuple-element.6, bf16[512,4,2,64]{0,3,2,1:T(8,128)(2,1)} %get-tuple-element.5, bf16[4,512,128]{2,1,0:T(8,128)(2,1)} %copy.19, bf16[4,512,128]{2,1,0:T(8,128)(2,1)} %copy-done.17, ...), kind=kOutput, calls=%fused_computation.3 | convolution fusion | flops 2181033984 | bytes 37765120 | tf_op jit(solution)/shard_map/rkgd,kld->kgrl/dot_general | solution.py:87
  231.1 15.1 %fusion.31 = bf16[512,4,2,128]{0,3,2,1:T(8,128)(2,1)} fusion(f32[4,2048,512,2]{2,1,3,0:T(8,128)} %get-tuple-element.22, pred[512,2048]{0,1:T(8,128)(4,1)S(1)} %copy-done.9, bf16[4,512,128]{1,2,0:T(8,128)(2,1)} %fusion.58, bf16[4,512,128]{1,2,0:T(8,128)(2,1)S(1)} %copy-done.16, bf16[4,1024,128]{1,2,0:T(8,128)(2,1)S(1)} %bitcast.147, ...), kind=kOutput, calls=%fused_computation.38 | convolution fusion | flops 2179989504 | bytes 37765120 | tf_op jit(solution)/shard_map/kgrl,kld->kgrd/dot_general | solution.py:93
  246.3 7.6 %fusion.19 = bf16[512,2688]{1,0:T(8,128)(2,1)} fusion(bf16[512,1024]{0,1:T(8,128)(2,1)} %bitcast.162, bf16[1,1024,2688]{2,1,0:T(8,128)(2,1)} %param.20), kind=kOutput, calls=%fused_computation.21 | convolution fusion | flops 2819948544 | bytes 9306112 | tf_op jit(solution)/shard_map/dot_general | solution.py:146
  253.9 54.0 %reduce-scatter.5.cloned.1.call-done = bf16[128,2688]{1,0:T(8,128)(2,1)} async-done(((bf16[512,2688]{1,0:T(8,128)(2,1)}), bf16[128,2688]{1,0:T(8,128)(2,1)}) %reduce-scatter.5.cloned.1.call-update) | async-done | bytes 688144 | tf_op jit(solution)/shard_map/reduce_scatter | solution.py:145
  (100 shorter events, 18.0 us)
Async XLA Ops:
  6.5 140.1 %reduce-scatter.3.cloned.1.call-start = ((), (), s32[]{:S(2)}) async-start(), calls=%async_computation.2 | async-start | bytes 3440640 | tf_op jit(solution)/shard_map/reduce_scatter | solution.py:145
  6.5 33.2 %collective-permute-start = (bf16[128,2688]{1,0:T(8,128)(2,1)}, bf16[128,2688]{1,0:T(8,128)(2,1)S(1)}, u32[]{:S(2)}, u32[]{:S(2)}) collective-permute-start(bf16[128,2688]{1,0:T(8,128)(2,1)} %bitcast.144), channel_id=1, source_target_pairs={{0,1},{1,2},{2,3},{3,0},{4,5},{5,6},{6,7},{7,4},{8,9},{9,10},{10,1... | collective-permute-start | bytes 2064392 | tf_op jit(solution)/shard_map/ppermute | solution.py:29
  9.5 35.2 %collective-permute-start.2 = (bf16[128,2688]{1,0:T(8,128)(2,1)}, bf16[128,2688]{1,0:T(8,128)(2,1)S(1)}, u32[]{:S(2)}, u32[]{:S(2)}) collective-permute-start(bf16[128,2688]{1,0:T(8,128)(2,1)} %bitcast.145), channel_id=1, source_target_pairs={{1,0},{2,1},{3,2},{0,3},{5,4},{6,5},{7,6},{4,7},{9,8},{10,9},{11,1... | collective-permute-start | bytes 2064392 | tf_op jit(solution)/shard_map/ppermute | solution.py:31
  25.5 14.1 %copy-start.18 = (f32[1,2688]{1,0:T(1,128)S(1)}, f32[1,2688]{1,0:T(1,128)}, u32[]{:S(2)}) copy-start(f32[1,2688]{1,0:T(1,128)} %param.14) | copy-start | bytes 32260
  25.5 32.3 %copy-start.2 = (bf16[1,128,2688]{2,1,0:T(8,128)(2,1)S(1)}, bf16[1,128,2688]{2,1,0:T(8,128)(2,1)}, u32[]{:S(2)}) copy-start(bf16[1,128,2688]{2,1,0:T(8,128)(2,1)} %param.11) | copy-start | bytes 2064388
  39.8 18.0 %copy-start.12 = (bf16[128,2688]{1,0:T(8,128)(2,1)}, bf16[128,2688]{1,0:T(8,128)(2,1)S(1)}, u32[]{:S(2)}) copy-start(bf16[128,2688]{1,0:T(8,128)(2,1)S(1)} %collective-permute-done) | copy-start | bytes 2064388
  39.8 18.0 %collective-permute-start.1 = (bf16[128,2688]{1,0:T(8,128)(2,1)S(1)}, bf16[128,2688]{1,0:T(8,128)(2,1)S(1)}, u32[]{:S(2)}, u32[]{:S(2)}) collective-permute-start(bf16[128,2688]{1,0:T(8,128)(2,1)S(1)} %collective-permute-done), channel_id=1, source_target_pairs={{0,1},{1,2},{2,3},{3,0},{4,5},{5,6},{6,7},{7,4},{8,9},{9,10},{10,1... | collective-permute-start | bytes 2064392 | tf_op jit(solution)/shard_map/ppermute | solution.py:29
  44.7 13.1 %copy-start.13 = (bf16[128,2688]{1,0:T(8,128)(2,1)}, bf16[128,2688]{1,0:T(8,128)(2,1)S(1)}, u32[]{:S(2)}) copy-start(bf16[128,2688]{1,0:T(8,128)(2,1)S(1)} %collective-permute-done.2) | copy-start | bytes 2064388
  73.0 0.7 copy-start.21
  73.4 16.1 %copy-start.15 = (bf16[4,512,128]{1,2,0:T(8,128)(2,1)}, bf16[4,512,128]{1,2,0:T(8,128)(2,1)S(1)}, u32[]{:S(2)}) copy-start(bf16[4,512,128]{1,2,0:T(8,128)(2,1)S(1)} %fusion.57) | copy-start | bytes 1572868
  73.6 0.9 copy-start.5
  73.6 1.0 copy-start.6
  75.9 1.1 copy-start.10
  76.4 13.1 %copy-start.17 = (bf16[4,512,128]{2,1,0:T(8,128)(2,1)}, bf16[4,512,128]{2,1,0:T(8,128)(2,1)S(1)}, u32[]{:S(2)}) copy-start(bf16[4,512,128]{2,1,0:T(8,128)(2,1)S(1)} %copy.13) | copy-start | bytes 1572868
  77.0 12.5 %copy-start.7 = (bf16[1,4,1024,128]{2,3,1,0:T(8,128)(2,1)S(1)}, bf16[1,4,1024,128]{2,3,1,0:T(8,128)(2,1)}, u32[]{:S(2)}) copy-start(bf16[1,4,1024,128]{2,3,1,0:T(8,128)(2,1)} %copy.15) | copy-start | bytes 3145732
  77.0 23.5 %slice-start = ((s8[5505024]{0:T(1024)(128)(4,1)}), s8[4194304]{0:T(1024)(128)(4,1)S(1)}, s32[]{:S(2)}) async-start(s8[5505024]{0:T(1024)(128)(4,1)} %bitcast.158), calls=%async_computation.4 | async-start | bytes 8388608
  89.5 11.0 %slice-start.1 = ((s8[5505024]{0:T(1024)(128)(4,1)}), s8[1310720]{0:T(1024)(128)(4,1)S(1)}, s32[]{:S(2)}) async-start(s8[5505024]{0:T(1024)(128)(4,1)} %bitcast.158), calls=%async_computation.5 | async-start | bytes 2621440
  105.3 0.7 copy-start.19
  105.3 47.4 %copy-start.11 = (bf16[1,128,2688]{2,1,0:T(8,128)(2,1)S(1)}, bf16[1,128,2688]{2,1,0:T(8,128)(2,1)}, u32[]{:S(2)}) copy-start(bf16[1,128,2688]{2,1,0:T(8,128)(2,1)} %param.12) | copy-start | bytes 2064388
  105.3 202.6 %reduce-scatter.5.cloned.1.call-start = ((), (), s32[]{:S(2)}) async-start(), calls=%async_computation.3 | async-start | bytes 3440640 | tf_op jit(solution)/shard_map/reduce_scatter | solution.py:145
  149.4 45.1 %copy-start = (bf16[128,2688]{1,0:T(8,128)(2,1)}, bf16[128,2688]{1,0:T(8,128)(2,1)S(1)}, u32[]{:S(2)}) copy-start(bf16[128,2688]{1,0:T(8,128)(2,1)S(1)} %fusion.45) | copy-start | bytes 2064388
  149.4 3.3 %collective-permute-start.3 = (bf16[128,2688]{1,0:T(8,128)(2,1)S(1)}, bf16[128,2688]{1,0:T(8,128)(2,1)S(1)}, u32[]{:S(2)}, u32[]{:S(2)}) collective-permute-start(bf16[128,2688]{1,0:T(8,128)(2,1)S(1)} %fusion.45), channel_id=1, source_target_pairs={{0,4},{4,8},{8,12},{12,16},{16,20},{20,24},{24,28},{1,5},{5,9},{9,... | collective-permute-start | bytes 2064392 | tf_op jit(solution)/shard_map/ppermute | solution.py:41
  152.8 12.2 %collective-permute-start.4 = (bf16[128,2688]{1,0:T(8,128)(2,1)S(1)}, bf16[128,2688]{1,0:T(8,128)(2,1)S(1)}, u32[]{:S(2)}, u32[]{:S(2)}) collective-permute-start(bf16[128,2688]{1,0:T(8,128)(2,1)S(1)} %bitcast_select_fusion.2), channel_id=1, source_target_pairs={{0,1},{1,2},{2,3},{3,0},{4,5},{5,6},{6,7},{7,4},{8,9},{9,10},{10,1... | collective-permute-start | bytes 2064392 | tf_op jit(solution)/shard_map/ppermute | solution.py:29
  154.3 25.4 %collective-permute-start.6 = (bf16[128,2688]{1,0:T(8,128)(2,1)S(1)}, bf16[128,2688]{1,0:T(8,128)(2,1)S(1)}, u32[]{:S(2)}, u32[]{:S(2)}) collective-permute-start(bf16[128,2688]{1,0:T(8,128)(2,1)S(1)} %bitcast_select_fusion.2), channel_id=1, source_target_pairs={{1,0},{2,1},{3,2},{0,3},{5,4},{6,5},{7,6},{4,7},{9,8},{10,9},{11,1... | collective-permute-start | bytes 2064392 | tf_op jit(solution)/shard_map/ppermute | solution.py:31
  165.0 29.5 %copy-start.14 = (bf16[128,2688]{1,0:T(8,128)(2,1)}, bf16[128,2688]{1,0:T(8,128)(2,1)S(1)}, u32[]{:S(2)}) copy-start(bf16[128,2688]{1,0:T(8,128)(2,1)S(1)} %collective-permute-done.4) | copy-start | bytes 2064388
  165.0 29.5 %collective-permute-start.5 = (bf16[128,2688]{1,0:T(8,128)(2,1)S(1)}, bf16[128,2688]{1,0:T(8,128)(2,1)S(1)}, u32[]{:S(2)}, u32[]{:S(2)}) collective-permute-start(bf16[128,2688]{1,0:T(8,128)(2,1)S(1)} %collective-permute-done.4), channel_id=1, source_target_pairs={{0,1},{1,2},{2,3},{3,0},{4,5},{5,6},{6,7},{7,4},{8,9},{9,10},{10,1... | collective-permute-start | bytes 2064392 | tf_op jit(solution)/shard_map/ppermute | solution.py:29
  210.8 0.9 copy-start.3
  210.8 1.0 copy-start.4
  213.1 1.2 copy-start.9
  214.4 16.8 %copy-start.8 = (bf16[1,4,1024,128]{2,3,1,0:T(8,128)(2,1)S(1)}, bf16[1,4,1024,128]{2,3,1,0:T(8,128)(2,1)}, u32[]{:S(2)}) copy-start(bf16[1,4,1024,128]{2,3,1,0:T(8,128)(2,1)} %copy.15) | copy-start | bytes 3145732
  214.4 16.8 %copy-start.16 = (bf16[4,512,128]{1,2,0:T(8,128)(2,1)S(1)}, bf16[4,512,128]{1,2,0:T(8,128)(2,1)}, u32[]{:S(2)}) copy-start(bf16[4,512,128]{1,2,0:T(8,128)(2,1)} %copy-done.15) | copy-start | bytes 1572868
  253.9 56.8 %copy-start.1 = (bf16[128,2688]{1,0:T(8,128)(2,1)S(1)}, bf16[128,2688]{1,0:T(8,128)(2,1)}, u32[]{:S(2)}) copy-start(bf16[128,2688]{1,0:T(8,128)(2,1)} %copy-done) | copy-start | bytes 2064388
  (1 other events, 0.7 us)
Sparse Core Ops, SparseCore 0:
  105.4 41.1 reduce-scatter.2
  254.0 53.8 reduce-scatter.4
